TPU v7x, 32 devices: a whole 2x2x4 slice. The times are simulated.
32 devices in a mesh: rep: 16 (over z, x, core), shard: 2 (over y).
Axes of the slice: x: 2, y: 2, z: 4, core: 2. Of those that a mesh axis runs over, the one named last changes fastest.
Arguments:
- tokens: bfloat16 [32, 197, 512], P(('rep', 'shard')), may hold values from -6 to 6
- norm_one: bfloat16 [512], P('shard'), may hold values from 0.099609375 to 1.8984375
- w_qkv: bfloat16 [512, 1536], P('shard'), may hold values from -0.25 to 0.25
- w_attn: bfloat16 [512, 512], P('shard'), may hold values from -1 to 1
- norm_two: bfloat16 [512], P('shard'), may hold values from 0.099609375 to 1.8984375
- w_gate: bfloat16 [512, 4], P('shard'), may hold values from -0.1875 to 0.1875
- w_expin: bfloat16 [4, 512, 2048], P(None, 'shard'), may hold values from -0.25 to 0.25
- w_expout: bfloat16 [4, 2048, 512], P(None, 'shard'), may hold values from -0.125 to 0.125
- routes: int32 [32, 197, 2], P(('rep', 'shard')), may hold values from 0 to 3, all different within a row
- cotangent: bfloat16 [32, 197, 512], P(('rep', 'shard')), may hold values from -6 to 6
Outputs:
- output: bfloat16 [32, 197, 512], P(('rep', 'shard'))
- grad_tokens: bfloat16 [32, 197, 512], P(('rep', 'shard'))
- grad_norm_one: float32 [512], P('shard')
- grad_qkv: float32 [512, 1536], P('shard')
- grad_attn: float32 [512, 512], P('shard')
- grad_norm_two: float32 [512], P('shard')
- grad_gate: float32 [512, 4], P('shard')
- grad_expin: float32 [4, 512, 2048], P(None, 'shard')
- grad_expout: float32 [4, 2048, 512], P(None, 'shard')
Inputs may be any that keep to these rules, and one draw needn't show every extreme that they name: `routes`: each token names two different experts; every expert is named by some token.
All inputs are finite; a program needn't handle non-finite values.
Results may differ from a plain program's by a relative error of at most 0.024.
Values may be sent and summed in bfloat16 or wider, within the bound.
A program may use at most 192 MiB of HBM per device.

v0:
```python
from functools import partial
import jax
import jax.numpy as jnp
from jax import lax
from jax.sharding import PartitionSpec as P

HEADS = 8
HEAD_DIM = 64
norm_eps = 1e-06
highest = lax.Precision.HIGHEST
fdt = jnp.float32
bdt = jnp.bfloat16


def layer_norm(inputs, gain_vec):
    centre = inputs - jnp.mean(inputs, axis=-1, keepdims=True)
    variance = jnp.mean(centre * centre, axis=-1, keepdims=True)
    inv_root = lax.rsqrt(variance + norm_eps)
    normed = centre * inv_root
    return (normed * gain_vec, normed, inv_root)


def norm_back(grad_out, normed, inv_root, gain_vec):
    scaled = grad_out * gain_vec
    back = inv_root * (
        scaled
        - jnp.mean(scaled, axis=-1, keepdims=True)
        - normed * jnp.mean(scaled * normed, axis=-1, keepdims=True)
    )
    return (back, jnp.sum(grad_out * normed, axis=0))


def forward(weights, tokens, routes, kept_total):
    norm_one, w_qkv, w_attn, norm_two, w_gate, w_expin, w_expout = weights
    images, seq_len, model_width = tokens.shape
    tok_rows = images * seq_len
    resid = tokens.reshape(tok_rows, model_width).astype(fdt)
    hidden_one, normed_one, root_one = layer_norm(resid, norm_one.astype(fdt))
    hidden_one_low = hidden_one.astype(bdt)
    proj = jnp.dot(hidden_one_low, w_qkv, preferred_element_type=fdt).astype(bdt)
    proj = proj.reshape(images, seq_len, 3, HEADS, HEAD_DIM)
    queries = proj[:, :, 0]
    key_rows = proj[:, :, 1]
    val_rows = proj[:, :, 2]
    score_scale = HEAD_DIM ** (-0.5)
    scores = (
        jnp.einsum("ishd,ithd->ihst", queries, key_rows, preferred_element_type=fdt) * score_scale
    )
    if kept_total is None:
        log_total = jax.nn.logsumexp(scores, axis=-1, keepdims=True)
    else:
        log_total = kept_total
    soft_probs = jnp.exp(scores - log_total)
    probs_low = soft_probs.astype(bdt)
    attn_rows = jnp.einsum("ihst,ithd->ishd", probs_low, val_rows, preferred_element_type=fdt)
    attn_rows = attn_rows.reshape(tok_rows, model_width).astype(bdt)
    mixed = resid + jnp.dot(attn_rows, w_attn, preferred_element_type=fdt)
    gate_gain = norm_two.astype(fdt)
    hidden_two, normed_two, root_two = layer_norm(mixed, gate_gain)
    router = w_gate.astype(fdt)
    logits = jnp.dot(hidden_two, router, precision=highest)
    expert_count = router.shape[1]
    choose = (
        routes.reshape(tok_rows, 2)[:, :, None] == jnp.arange(expert_count)[None, None, :]
    ).astype(fdt)
    picked = jnp.sum(choose * logits[:, None, :], axis=-1)
    gates = jax.nn.softmax(picked, axis=-1)
    weight_map = jnp.sum(gates[:, :, None] * choose, axis=1)
    hidden_two_low = hidden_two.astype(bdt)
    expert_inner = jnp.einsum("td,edf->etf", hidden_two_low, w_expin, preferred_element_type=fdt)
    hidden_act = jax.nn.gelu(expert_inner, approximate=False).astype(bdt)
    outer = jnp.einsum("etf,efd->etd", hidden_act, w_expout, preferred_element_type=fdt)
    combined = mixed + jnp.sum(weight_map.T[:, :, None] * outer, axis=0)
    return {
        "combined": combined,
        "log_total": log_total,
        "resid": resid,
        "normed_one": normed_one,
        "root_one": root_one,
        "hidden_one_low": hidden_one_low,
        "queries": queries,
        "key_rows": key_rows,
        "val_rows": val_rows,
        "soft_probs": soft_probs,
        "probs_low": probs_low,
        "attn_rows": attn_rows,
        "normed_two": normed_two,
        "root_two": root_two,
        "hidden_two": hidden_two,
        "hidden_two_low": hidden_two_low,
        "choose": choose,
        "gates": gates,
        "weight_map": weight_map,
        "expert_inner": expert_inner,
        "hidden_act": hidden_act,
        "outer": outer,
    }


def on_device(
    tokens, norm_one, w_qkv, w_attn, norm_two, w_gate, w_expin, w_expout, routes, cotangent
):
    images, seq_len, model_width = tokens.shape
    tok_rows = images * seq_len
    whole = (
        lax.all_gather(norm_one, "shard", axis=0, tiled=True),
        lax.all_gather(w_qkv, "shard", axis=0, tiled=True),
        lax.all_gather(w_attn, "shard", axis=0, tiled=True),
        lax.all_gather(norm_two, "shard", axis=0, tiled=True),
        lax.all_gather(w_gate, "shard", axis=0, tiled=True),
        lax.all_gather(w_expin, "shard", axis=1, tiled=True),
        lax.all_gather(w_expout, "shard", axis=1, tiled=True),
    )
    first = forward(whole, tokens, routes, None)
    output = first["combined"].reshape(images, seq_len, model_width).astype(bdt)
    again = (
        lax.all_gather(norm_one, "shard", axis=0, tiled=True),
        lax.all_gather(w_qkv, "shard", axis=0, tiled=True),
        lax.all_gather(w_attn, "shard", axis=0, tiled=True),
        lax.all_gather(norm_two, "shard", axis=0, tiled=True),
        lax.all_gather(w_gate, "shard", axis=0, tiled=True),
        lax.all_gather(w_expin, "shard", axis=1, tiled=True),
        lax.all_gather(w_expout, "shard", axis=1, tiled=True),
    )
    parts = forward(again, tokens, routes, first["log_total"])
    g_one, m_qkv, m_attn, g_two, m_gate, m_expin, m_expout = again
    gain_one = g_one.astype(fdt)
    gain_two = g_two.astype(fdt)
    router = m_gate.astype(fdt)
    dout = cotangent.reshape(tok_rows, model_width).astype(fdt)
    dweight = jnp.sum(dout[None, :, :] * parts["outer"], axis=-1).T
    dout_exp = (parts["weight_map"].T[:, :, None] * dout[None, :, :]).astype(bdt)
    grad_expout = jnp.einsum(
        "etf,etd->efd", parts["hidden_act"], dout_exp, preferred_element_type=fdt
    )
    dhidden = jnp.einsum("etd,efd->etf", dout_exp, m_expout, preferred_element_type=fdt)
    gelu_exact = partial(jax.nn.gelu, approximate=False)
    _, gelu_pull = jax.vjp(gelu_exact, parts["expert_inner"])
    dinner = gelu_pull(dhidden)[0].astype(bdt)
    grad_expin = jnp.einsum(
        "td,etf->edf", parts["hidden_two_low"], dinner, preferred_element_type=fdt
    )
    dhidden_two = jnp.einsum("etf,edf->td", dinner, m_expin, preferred_element_type=fdt)
    choose = parts["choose"]
    gates = parts["gates"]
    dpicked = jnp.sum(choose * dweight[:, None, :], axis=-1)
    gate_dot = jnp.sum(gates * dpicked, axis=-1, keepdims=True)
    dpair = gates * (dpicked - gate_dot)
    dlogits = jnp.sum(dpair[:, :, None] * choose, axis=1)
    grad_gate = jnp.dot(parts["hidden_two"].T, dlogits, precision=highest)
    dhidden_two = dhidden_two + jnp.dot(dlogits, router.T, precision=highest)
    dmixed_norm, grad_norm_two = norm_back(
        dhidden_two, parts["normed_two"], parts["root_two"], gain_two
    )
    dmixed = dout + dmixed_norm
    dmixed_low = dmixed.astype(bdt)
    grad_attn = jnp.dot(parts["attn_rows"].T, dmixed_low, preferred_element_type=fdt)
    dattn = jnp.dot(dmixed_low, m_attn.T, preferred_element_type=fdt).astype(bdt)
    dattn = dattn.reshape(images, seq_len, HEADS, HEAD_DIM)
    dprobs = jnp.einsum("ishd,ithd->ihst", dattn, parts["val_rows"], preferred_element_type=fdt)
    dvalues = jnp.einsum("ihst,ishd->ithd", parts["probs_low"], dattn, preferred_element_type=fdt)
    soft_probs = parts["soft_probs"]
    row_delta = jnp.sum(dprobs * soft_probs, axis=-1, keepdims=True)
    dscores = (soft_probs * (dprobs - row_delta)).astype(bdt)
    score_scale = HEAD_DIM ** (-0.5)
    dqueries = (
        jnp.einsum("ihst,ithd->ishd", dscores, parts["key_rows"], preferred_element_type=fdt)
        * score_scale
    )
    dkeys = (
        jnp.einsum("ihst,ishd->ithd", dscores, parts["queries"], preferred_element_type=fdt)
        * score_scale
    )
    dproj = (
        jnp.stack([dqueries, dkeys, dvalues], axis=2).reshape(tok_rows, 3 * model_width).astype(bdt)
    )
    grad_qkv = jnp.dot(parts["hidden_one_low"].T, dproj, preferred_element_type=fdt)
    dhidden_one = jnp.dot(dproj, m_qkv.T, preferred_element_type=fdt)
    dresid_norm, grad_norm_one = norm_back(
        dhidden_one, parts["normed_one"], parts["root_one"], gain_one
    )
    grad_tokens = (dmixed + dresid_norm).reshape(images, seq_len, model_width).astype(bdt)
    owned = (
        lax.psum_scatter(
            grad_norm_one.astype(jnp.bfloat16), "shard", scatter_dimension=0, tiled=True
        ).astype(jnp.float32),
        lax.psum_scatter(
            grad_qkv.astype(jnp.bfloat16), "shard", scatter_dimension=0, tiled=True
        ).astype(jnp.float32),
        lax.psum_scatter(
            grad_attn.astype(jnp.bfloat16), "shard", scatter_dimension=0, tiled=True
        ).astype(jnp.float32),
        lax.psum_scatter(
            grad_norm_two.astype(jnp.bfloat16), "shard", scatter_dimension=0, tiled=True
        ).astype(jnp.float32),
        lax.psum_scatter(
            grad_gate.astype(jnp.bfloat16), "shard", scatter_dimension=0, tiled=True
        ).astype(jnp.float32),
        lax.psum_scatter(
            grad_expin.astype(jnp.bfloat16), "shard", scatter_dimension=1, tiled=True
        ).astype(jnp.float32),
        lax.psum_scatter(
            grad_expout.astype(jnp.bfloat16), "shard", scatter_dimension=1, tiled=True
        ).astype(jnp.float32),
    )
    summed = (
        lax.psum(owned[0].astype(jnp.bfloat16), "rep").astype(jnp.float32),
        lax.psum(owned[1].astype(jnp.bfloat16), "rep").astype(jnp.float32),
        lax.psum(owned[2].astype(jnp.bfloat16), "rep").astype(jnp.float32),
        lax.psum(owned[3].astype(jnp.bfloat16), "rep").astype(jnp.float32),
        lax.psum(owned[4].astype(jnp.bfloat16), "rep").astype(jnp.float32),
        lax.psum(owned[5].astype(jnp.bfloat16), "rep").astype(jnp.float32),
        lax.psum(owned[6].astype(jnp.bfloat16), "rep").astype(jnp.float32),
    )
    return (
        output,
        grad_tokens,
        summed[0],
        summed[1],
        summed[2],
        summed[3],
        summed[4],
        summed[5],
        summed[6],
    )


def solution(mesh):
    placed = (
        P(("rep", "shard"), None, None),
        P("shard"),
        P("shard", None),
        P("shard", None),
        P("shard"),
        P("shard", None),
        P(None, "shard", None),
        P(None, "shard", None),
        P(("rep", "shard"), None, None),
        P(("rep", "shard"), None, None),
    )
    return jax.shard_map(
        on_device,
        mesh=mesh,
        in_specs=placed,
        out_specs=(
            P(("rep", "shard"), None, None),
            P(("rep", "shard"), None, None),
            P("shard"),
            P("shard", None),
            P("shard", None),
            P("shard"),
            P("shard", None),
            P(None, "shard", None),
            P(None, "shard", None),
        ),
        check_vma=False,
    )
```

profile of v0, /device:TPU:0, one launch (start us, length us, event | category | flops | bytes accessed | tf_op | source)
XLA Modules:
  0.0 764.5 jit_solution(5038029769242780368)
XLA Ops:
  7.3 0.7 all-gather.6.cloned.1.call-update
  8.0 0.7 all-gather.8.cloned.1.call-update
  8.8 0.7 all-gather.10.cloned.1.call-update
  9.5 0.1 convert_reduce_fusion
  9.7 5.2 all-gather
  14.8 4.2 all-gather.1
  19.1 4.3 all_gather.32
  23.4 0.2 fusion.43
  23.7 14.0 %all_gather.30 = bf16[512,512]{1,0:T(8,128)(2,1)} all-gather(bf16[256,512]{1,0:T(8,128)(2,1)S(1)} %copy-done.11), channel_id=1, replica_groups=mesh['rep'=16,'shard'=2] {'shard'}, dimensions={0}, use_global_device_ids=true | all-gather | bytes 786432 | tf_op jit(solution)/shard_map/all_gather | solution.py:108
  37.7 0.8 bitcast_convert_fusion
  38.5 6.7 all-gather.6.cloned.1.call-done
  45.2 1.9 convolution_convert_fusion.2
  47.2 0.3 copy.50
  47.4 0.4 fusion.75
  47.9 0.3 exponential_reduce_fusion
  48.2 0.4 convolution_convert_fusion.4
  48.6 0.7 copy-done.3
  49.3 1.4 fusion.76
  50.7 0.2 multiply_reduce_fusion.5
  50.9 0.4 fusion.48
  51.5 99.3 %all-gather.8.cloned.1.call-done = bf16[4,512,2048]{2,1,0:T(8,128)(2,1)} async-done(((bf16[4,256,2048]{2,1,0:T(8,128)(2,1)}), bf16[4,512,2048]{2,1,0:T(8,128)(2,1)}) %all-gather.8.cloned.1.call-update) | async-done | bytes 8388624 | tf_op jit(solution)/shard_map/all_gather | solution.py:111
  150.8 18.8 %fusion.2 = (bf16[4,197,2048]{2,1,0:T(8,128)(2,1)}, f32[4,197,2048]{2,1,0:T(8,128)}, f32[197,4,2048]{2,0,1:T(8,128)}) fusion(bf16[4,512,2048]{2,1,0:T(8,128)(2,1)} %all-gather.8.cloned.1.call-done, f32[512]{0:T(512)S(1)} %bitcast.219, f32[197]{0:T(256)S(1)} %add_rsqrt_fusion, f32[197,512]{1,0:T(8,128)S(1)} %get-tuple-element.69, ...), kind=kOutput, calls=%fused_computation.10 | convolution fusion | flops 1757857792 | bytes 24933928 | tf_op jit(solution)/shard_map/td,edf->etf/dot_general | solution.py:70
  169.6 86.8 %all-gather.10.cloned.1.call-done = bf16[4,2048,512]{2,1,0:T(8,128)(2,1)} async-done(((bf16[4,1024,512]{2,1,0:T(8,128)(2,1)}), bf16[4,2048,512]{2,1,0:T(8,128)(2,1)}) %all-gather.10.cloned.1.call-update) | async-done | bytes 8388624 | tf_op jit(solution)/shard_map/all_gather | solution.py:112
  256.4 6.5 multiply_reduce_fusion.1
  263.0 11.2 %fusion.8 = bf16[4,197,2048]{2,1,0:T(8,128)(2,1)S(1)} fusion(f32[4,197,2048]{2,1,0:T(8,128)} %get-tuple-element.63, f32[197,4,2048]{2,0,1:T(8,128)} %get-tuple-element.70, bf16[4,2048,512]{2,1,0:T(8,128)(2,1)} %all-gather.10.cloned.1.call-done, f32[197,512]{1,0:T(8,128)S(1)} %copy-done.6, f32[4,197]{1,0:T(4,128)S(1)} %bitcast.233), kind=kOutput, calls=%fused_computation.16 | convolution fusion | flops 1675956224 | bytes 24933456 | tf_op jit(solution)/shard_map/etd,efd->etf/dot_general | solution.py:136
  274.3 7.4 convolution_bitcast_fusion.1
  281.7 0.6 multiply_reduce_fusion.3
  282.3 0.8 multiply_add_fusion
  283.1 1.0 convolution_convert_fusion.5
  284.1 1.1 convolution_convert_fusion.3
  285.2 1.8 copy.52
  287.0 2.6 multiply_reduce_fusion
  289.6 0.3 reduce-scatter.8.cloned.1.call-start
  289.9 1.9 multiply_convert_fusion
  291.7 0.4 fusion.22
  292.1 0.3 fusion.23
  292.4 0.4 convolution_bitcast_fusion
  292.8 0.2 maximum_convert_fusion
  293.0 1.9 convolution_convert_fusion.1
  295.0 8.1 %convert_bitcast_fusion = bf16[4,512,2048]{1,2,0:T(8,128)(2,1)} fusion(bf16[4,197,2048]{2,1,0:T(8,128)(2,1)} %copy-done.1, f32[512]{0:T(512)S(1)} %bitcast.222, f32[197,512]{1,0:T(8,128)S(1)} %get-tuple-element.69, f32[197]{0:T(256)S(1)} %add_rsqrt_fusion, f32[197]{0:T(256)S(1)} %broadcast_multiply_fusion.4), kind=kOutput, calls=%fused_computation.1 | convolution fusion | flops 1657153536 | bytes 12023336 | tf_op jit(solution)/shard_map/td,etf->edf/dot_general | solution.py:140
  303.2 0.9 copy-done.7
  304.1 7.9 %convolution_convert_fusion = bf16[4,2048,512]{2,1,0:T(8,128)(2,1)} fusion(bf16[4,197,2048]{2,1,0:T(8,128)(2,1)} %get-tuple-element.62, f32[197,512]{1,0:T(8,128)S(1)} %copy-done.7, f32[4,197]{1,0:T(4,128)S(1)} %bitcast.234), kind=kOutput, calls=%fused_computation.30 | convolution fusion | flops 1657556992 | bytes 12022864 | tf_op jit(solution)/shard_map/etf,etd->efd/dot_general | solution.py:133
  312.0 0.5 convolution_convert_fusion.6
  312.5 0.8 copy.61
  313.4 19.7 %reduce-scatter.8.cloned.1.call-done = bf16[256,1536]{1,0:T(8,128)(2,1)} async-done(((bf16[512,1536]{1,0:T(8,128)(2,1)}), bf16[256,1536]{1,0:T(8,128)(2,1)}) %reduce-scatter.8.cloned.1.call-update) | async-done | bytes 786448 | tf_op jit(solution)/shard_map/reduce_scatter | solution.py:187
  333.2 102.0 %reduce-scatter.12.cloned.1.call-done = bf16[4,256,2048]{1,2,0:T(8,128)(2,1)} async-done(((bf16[4,512,2048]{1,2,0:T(8,128)(2,1)}), bf16[4,256,2048]{1,2,0:T(8,128)(2,1)}) %reduce-scatter.12.cloned.1.call-update) | async-done | bytes 4194320 | tf_op jit(solution)/shard_map/reduce_scatter | solution.py:199
  435.2 102.2 %reduce-scatter.14.cloned.1.call-done = bf16[4,1024,512]{2,1,0:T(8,128)(2,1)} async-done(((bf16[4,2048,512]{2,1,0:T(8,128)(2,1)}), bf16[4,1024,512]{2,1,0:T(8,128)(2,1)}) %reduce-scatter.14.cloned.1.call-update) | async-done | bytes 4194320 | tf_op jit(solution)/shard_map/reduce_scatter | solution.py:202
  537.4 0.6 dynamic-slice
  538.7 0.8 fusion.42
  539.5 4.9 all-reduce.4
  544.4 0.1 dynamic-slice.1
  544.5 0.1 dynamic-slice.3
  544.6 0.9 fusion.57
  545.5 4.4 reduce-scatter.16.cloned.1.call-done
  549.9 0.9 copy.62
  550.9 34.5 %all-reduce.2 = (bf16[256]{0:T(256)(128)(2,1)S(1)}, bf16[256]{0:T(256)(128)(2,1)S(1)}, bf16[256,4]{0,1:T(4,128)(2,1)S(1)}) all-reduce(bf16[256]{0:T(256)(128)(2,1)S(1)} %dynamic-slice.1, bf16[256]{0:T(256)(128)(2,1)S(1)} %dynamic-slice.3, bf16[256,4]{0,1:T(4,128)(2,1)S(1)} %copy.62), channel_id=1, replica_groups=mesh['rep'=16,'shard'=2] {'rep'}, use_global_device_ids=true, to_apply=%region_22.0 | all-reduce | flops 1536 | bytes 6144 | tf_op jit(solution)/shard_map/psum | solution.py:207
  585.3 0.6 convert_element_type.202
  585.9 0.6 convert_element_type.210
  586.5 0.6 convert_element_type.212
  587.1 153.0 %all-reduce.7.cloned.1.call-done = (bf16[4,256,2048]{1,2,0:T(8,128)(2,1)}, bf16[256,1536]{1,0:T(8,128)(2,1)}, bf16[256,512]{1,0:T(8,128)(2,1)}, bf16[4,1024,512]{2,1,0:T(8,128)(2,1)}) async-done(((bf16[4,256,2048]{1,2,0:T(8,128)(2,1)}, bf16[256,1536]{1,0:T(8,128)(2,1)}, bf16[256,512]{1,0:T(8,128)(2,1)}, bf16[4,1024,512]{2,1,0:T(8,128)(2,1)}), (bf16[4,256,2048]{1,2,0:T(8,128)(2,1)}, ...) | async-done | bytes 9437200 | tf_op jit(solution)/shard_map/psum | solution.py:212
  740.0 2.5 convert_element_type.206
  742.5 1.8 convert_element_type.208
  744.3 6.9 copy.56
  751.2 6.8 convert_element_type.217
  (69 shorter events, 0.8 us)
Async XLA Ops:
  7.2 2.3 copy-start
  7.2 2.4 copy-start.14
  7.2 7.6 copy-start.15
  7.2 11.9 %copy-start.13 = (bf16[256,4]{0,1:T(4,128)(2,1)S(1)}, bf16[256,4]{0,1:T(4,128)(2,1)}, u32[]{:S(2)}) copy-start(bf16[256,4]{0,1:T(4,128)(2,1)} %param.15) | copy-start | bytes 6148
  7.2 16.4 %copy-start.11 = (bf16[256,512]{1,0:T(8,128)(2,1)S(1)}, bf16[256,512]{1,0:T(8,128)(2,1)}, u32[]{:S(2)}) copy-start(bf16[256,512]{1,0:T(8,128)(2,1)} %param.13) | copy-start | bytes 786436
  7.2 30.5 %copy-start.9 = (bf16[1,197,512]{2,1,0:T(8,128)(2,1)S(1)}, bf16[1,197,512]{2,1,0:T(8,128)(2,1)}, u32[]{:S(2)}) copy-start(bf16[1,197,512]{2,1,0:T(8,128)(2,1)} %param.19) | copy-start | bytes 605188
  7.2 38.0 %all-gather.6.cloned.1.call-start = ((), (), s32[]{:S(2)}) async-start(), calls=%async_computation.5 | async-start | bytes 2359296 | tf_op jit(solution)/shard_map/all_gather | solution.py:107
  8.0 142.8 %all-gather.8.cloned.1.call-start = ((), (), s32[]{:S(2)}) async-start(), calls=%async_computation.6 | async-start | bytes 12582912 | tf_op jit(solution)/shard_map/all_gather | solution.py:111
  8.7 247.7 %all-gather.10.cloned.1.call-start = ((), (), s32[]{:S(2)}) async-start(), calls=%async_computation.7 | async-start | bytes 12582912 | tf_op jit(solution)/shard_map/all_gather | solution.py:112
  9.5 304.0 %reduce-scatter.10.cloned.1.call-start = ((), (), s32[]{:S(2)}) async-start(), calls=%async_computation.9 | async-start | bytes 786432 | tf_op jit(solution)/shard_map/reduce_scatter | solution.py:190
  23.7 27.7 %copy-start.12 = (s32[1,197,2]{1,2,0:T(2,128)S(1)}, s32[1,197,2]{1,2,0:T(2,128)}, u32[]{:S(2)}) copy-start(s32[1,197,2]{1,2,0:T(2,128)} %param.18) | copy-start | bytes 4732
  48.6 0.7 copy-start.3
  51.5 204.9 %copy-start.6 = (f32[197,512]{1,0:T(8,128)S(1)}, f32[197,512]{1,0:T(8,128)}, u32[]{:S(2)}) copy-start(f32[197,512]{1,0:T(8,128)} %bitcast_convert_fusion) | copy-start | bytes 1210372
  274.2 7.5 copy-start.1
  274.2 8.1 %copy-start.10 = (bf16[1,197,512]{2,1,0:T(8,128)(2,1)S(1)}, bf16[1,197,512]{2,1,0:T(8,128)(2,1)}, u32[]{:S(2)}) copy-start(bf16[1,197,512]{2,1,0:T(8,128)(2,1)} %param.19) | copy-start | bytes 605188
  274.2 8.9 %copy-start.2 = (bf16[512,512]{1,0:T(8,128)(2,1)S(1)}, bf16[512,512]{1,0:T(8,128)(2,1)}, u32[]{:S(2)}) copy-start(bf16[512,512]{1,0:T(8,128)(2,1)} %all_gather.30) | copy-start | bytes 1572868
  274.2 9.9 %copy-start.4 = (bf16[8,64,197]{2,1,0:T(8,128)(2,1)S(1)}, bf16[8,64,197]{2,1,0:T(8,128)(2,1)}, u32[]{:S(2)}) copy-start(bf16[8,64,197]{2,1,0:T(8,128)(2,1)} %copy-done.3) | copy-start | bytes 605188
  289.6 43.6 %reduce-scatter.8.cloned.1.call-start = ((), (), s32[]{:S(2)}) async-start(), calls=%async_computation.8 | async-start | bytes 2359296 | tf_op jit(solution)/shard_map/reduce_scatter | solution.py:187
  289.8 2.6 copy-start.5
  294.9 140.2 %reduce-scatter.12.cloned.1.call-start = ((), (), s32[]{:S(2)}) async-start(), calls=%async_computation.10 | async-start | bytes 12582912 | tf_op jit(solution)/shard_map/reduce_scatter | solution.py:199
  303.1 1.0 copy-start.7
  303.1 234.3 %reduce-scatter.14.cloned.1.call-start = ((), (), s32[]{:S(2)}) async-start(), calls=%async_computation.11 | async-start | bytes 12582912 | tf_op jit(solution)/shard_map/reduce_scatter | solution.py:202
  312.0 225.4 %copy-start.16 = (u32[32]{0:T(128)S(1)}, u32[32]{0:T(128)}, u32[]{:S(2)}) copy-start(u32[32]{0:T(128)} %constant.92) | copy-start | bytes 388
  312.0 226.7 %copy-start.8 = (bf16[512,1536]{1,0:T(8,128)(2,1)S(1)}, bf16[512,1536]{1,0:T(8,128)(2,1)}, u32[]{:S(2)}) copy-start(bf16[512,1536]{1,0:T(8,128)(2,1)} %all-gather.6.cloned.1.call-done) | copy-start | bytes 4718596
  312.0 237.9 %reduce-scatter.16.cloned.1.call-start = ((), (), s32[]{:S(2)}) async-start(), calls=%async_computation.12 | async-start | bytes 196608
  313.3 426.7 %all-reduce.7.cloned.1.call-start = ((), (), s32[]{:S(2)}) async-start(), calls=%async_computation.13 | async-start | bytes 18874368 | tf_op jit(solution)/shard_map/psum | solution.py:212
Sparse Core Ops, SparseCore 0:
  9.6 35.5 all-gather.5
  46.7 103.9 all-gather.7
  152.3 103.9 all-gather.9
  289.7 14.5 reduce-scatter.9
  307.0 26.0 reduce-scatter.7
  335.9 99.2 reduce-scatter.11
  438.1 99.2 reduce-scatter.13
  539.6 10.2 reduce-scatter.15
  553.9 186.0 all-reduce.6
where the time goes:
time: 765 us; the launch traced here: 764 us
  waiting for transfers between devices  576 us (75%)
  matrix products  74.1 us (10%)
  blocking collectives  67.2 us (9%)
  other arithmetic  18.4 us (2%)
  between operations  14.8 us (2%)
  local copies, waits for them, and re-layouts  13.1 us (2%)
    psum x1, waiting for transfers between devices, on_device(): lax.psum(owned[5].astype(jnp.bfloat16), 'rep').astype(jnp.float32)  153 us
    reduce_scatter x1, waiting for transfers between devices, on_device(): lax.psum_scatter(grad_expout.astype(jnp.bfloat16), 'shard', scatter_dimen...  102 us
    reduce_scatter x1, waiting for transfers between devices, on_device(): lax.psum_scatter(grad_expin.astype(jnp.bfloat16), 'shard', scatter_dimens...  102 us
    all_gather x1, waiting for transfers between devices, on_device(): lax.all_gather(w_expin, 'shard', axis=1, tiled=True)  99.3 us
    all_gather x1, waiting for transfers between devices, on_device(): lax.all_gather(w_expout, 'shard', axis=1, tiled=True)  86.8 us
    psum x1, blocking collectives, on_device(): lax.psum(owned[0].astype(jnp.bfloat16), 'rep').astype(jnp.float32)  34.5 us
    reduce_scatter x1, waiting for transfers between devices, on_device(): lax.psum_scatter(grad_qkv.astype(jnp.bfloat16), 'shard', scatter_dimensio...  19.7 us
    dot_general x1, matrix products, forward(): jnp.einsum('td,edf->etf', hidden_two_low, w_expin, preferred_element_type...  18.8 us
  transfers between devices with their start and end apart: 9, of which 8 were waited for; matrix products, arithmetic and copies ran while one was open for 7% of the time, Pallas kernels for 0%

commit v1 on v0

--- a/solution.py
+++ b/solution.py
@@ -10,6 +10,12 @@
 highest = lax.Precision.HIGHEST
 fdt = jnp.float32
 bdt = jnp.bfloat16
+
+
+def add_all(block, name):
+    pieces = lax.all_gather(block, name, axis=0, tiled=False)
+    result = pieces.sum(axis=0)
+    return result
 
 
 def layer_norm(inputs, gain_vec):
@@ -209,7 +215,7 @@
         lax.psum(owned[2].astype(jnp.bfloat16), "rep").astype(jnp.float32),
         lax.psum(owned[3].astype(jnp.bfloat16), "rep").astype(jnp.float32),
         lax.psum(owned[4].astype(jnp.bfloat16), "rep").astype(jnp.float32),
-        lax.psum(owned[5].astype(jnp.bfloat16), "rep").astype(jnp.float32),
+        add_all(owned[5].astype(jnp.bfloat16), "rep").astype(jnp.float32),
         lax.psum(owned[6].astype(jnp.bfloat16), "rep").astype(jnp.float32),
     )
     return (

time: 765 us -> 1050 us (1.37)
  waiting for transfers between devices: 576 us -> 826 us
  other arithmetic: 18.4 us -> 42.8 us
  local copies, waits for them, and re-layouts: 13.1 us -> 24.5 us
    all_gather x0 -> x1, waiting for transfers between devices: none -> 315 us  [add_all(): pieces = lax.all_gather(block, name, axis=0, tiled=False)]
    psum x1, waiting for transfers between devices: 153 us -> 91.7 us  [on_device(): lax.psum(owned[1].astype(jnp.bfloat16), 'rep').astype(jnp.float32)]
    reduce_sum x0 -> x1, other arithmetic: none -> 23.8 us  [add_all(): result = pieces.sum(axis=0)]
  transfers between devices with their start and end apart: 9 -> 10, of which waited for: 8 -> 8; matrix products, arithmetic and copies ran while one was open for 7% -> 7% of each run, Pallas kernels for 0% -> 0%
where the time goes in v1:
time: 1050 us
  waiting for transfers between devices  826 us (79%)
  matrix products  73.1 us (7%)
  blocking collectives  66.5 us (6%)
  other arithmetic  42.8 us (4%)
  local copies, waits for them, and re-layouts  24.5 us (2%)
  between operations  15.2 us (1%)
    all_gather x1, waiting for transfers between devices, add_all(): pieces = lax.all_gather(block, name, axis=0, tiled=False)  315 us
    reduce_scatter x1, waiting for transfers between devices, on_device(): lax.psum_scatter(grad_expin.astype(jnp.bfloat16), 'shard', scatter_dimens...  102 us
    reduce_scatter x1, waiting for transfers between devices, on_device(): lax.psum_scatter(grad_expout.astype(jnp.bfloat16), 'shard', scatter_dimen...  102 us
    all_gather x1, waiting for transfers between devices, on_device(): lax.all_gather(w_expin, 'shard', axis=1, tiled=True)  99.3 us
    psum x1, waiting for transfers between devices, on_device(): lax.psum(owned[1].astype(jnp.bfloat16), 'rep').astype(jnp.float32)  91.7 us
    all_gather x1, waiting for transfers between devices, on_device(): lax.all_gather(w_expout, 'shard', axis=1, tiled=True)  86.8 us
    psum x1, blocking collectives, on_device(): lax.psum(owned[0].astype(jnp.bfloat16), 'rep').astype(jnp.float32)  33.8 us
    reduce_sum x1, other arithmetic, add_all(): result = pieces.sum(axis=0)  23.8 us
  transfers between devices with their start and end apart: 10, of which 8 were waited for; matrix products, arithmetic and copies ran while one was open for 7% of the time, Pallas kernels for 0%

profile of v1, /device:TPU:0, one launch (start us, length us, event | category | flops | bytes accessed | tf_op | source)
XLA Modules:
  0.0 1049.0 jit_solution(5029005607172778200)
XLA Ops:
  7.3 0.7 all-gather.8.cloned.1.call-update
  8.0 0.7 all-gather.10.cloned.1.call-update
  8.8 0.7 all-gather.12.cloned.1.call-update
  9.5 0.1 convert_reduce_fusion
  9.7 5.2 all-gather.1
  14.8 4.2 all-gather.2
  19.1 4.3 all_gather.38
  23.4 0.2 fusion.43
  23.7 14.0 %all_gather.36 = bf16[512,512]{1,0:T(8,128)(2,1)} all-gather(bf16[256,512]{1,0:T(8,128)(2,1)S(1)} %copy-done.10), channel_id=1, replica_groups=mesh['rep'=16,'shard'=2] {'shard'}, dimensions={0}, use_global_device_ids=true | all-gather | bytes 786432 | tf_op jit(solution)/shard_map/all_gather | solution.py:114
  37.7 0.8 bitcast_convert_fusion
  38.5 6.7 all-gather.8.cloned.1.call-done
  45.2 1.9 convolution_convert_fusion.2
  47.2 0.3 copy.50
  47.4 0.4 fusion.75
  47.9 0.3 exponential_reduce_fusion
  48.2 0.4 convolution_convert_fusion.4
  48.6 0.7 copy-done.3
  49.3 1.4 fusion.76
  50.7 0.2 multiply_reduce_fusion.5
  50.9 0.4 fusion.48
  51.5 99.3 %all-gather.10.cloned.1.call-done = bf16[4,512,2048]{2,1,0:T(8,128)(2,1)} async-done(((bf16[4,256,2048]{2,1,0:T(8,128)(2,1)}), bf16[4,512,2048]{2,1,0:T(8,128)(2,1)}) %all-gather.10.cloned.1.call-update) | async-done | bytes 8388624 | tf_op jit(solution)/shard_map/all_gather | solution.py:117
  150.8 18.8 %fusion.2 = (bf16[4,197,2048]{2,1,0:T(8,128)(2,1)}, f32[4,197,2048]{2,1,0:T(8,128)}, f32[197,4,2048]{2,0,1:T(8,128)}) fusion(bf16[4,512,2048]{2,1,0:T(8,128)(2,1)} %all-gather.10.cloned.1.call-done, f32[512]{0:T(512)S(1)} %bitcast.220, f32[197]{0:T(256)S(1)} %add_rsqrt_fusion, f32[197,512]{1,0:T(8,128)S(1)} %get-tuple-element.50, ...), kind=kOutput, calls=%fused_computation.10 | convolution fusion | flops 1757857792 | bytes 24933928 | tf_op jit(solution)/shard_map/td,edf->etf/dot_general | solution.py:76
  169.6 86.8 %all-gather.12.cloned.1.call-done = bf16[4,2048,512]{2,1,0:T(8,128)(2,1)} async-done(((bf16[4,1024,512]{2,1,0:T(8,128)(2,1)}), bf16[4,2048,512]{2,1,0:T(8,128)(2,1)}) %all-gather.12.cloned.1.call-update) | async-done | bytes 8388624 | tf_op jit(solution)/shard_map/all_gather | solution.py:118
  256.4 6.5 multiply_reduce_fusion.1
  263.0 11.2 %fusion.8 = bf16[4,197,2048]{2,1,0:T(8,128)(2,1)S(1)} fusion(f32[4,197,2048]{2,1,0:T(8,128)} %get-tuple-element.44, f32[197,4,2048]{2,0,1:T(8,128)} %get-tuple-element.51, bf16[4,2048,512]{2,1,0:T(8,128)(2,1)} %all-gather.12.cloned.1.call-done, f32[197,512]{1,0:T(8,128)S(1)} %copy-done.6, f32[4,197]{1,0:T(4,128)S(1)} %bitcast.234), kind=kOutput, calls=%fused_computation.16 | convolution fusion | flops 1675956224 | bytes 24933456 | tf_op jit(solution)/shard_map/etd,efd->etf/dot_general | solution.py:142
  274.3 7.4 convolution_bitcast_fusion.1
  281.7 0.6 multiply_reduce_fusion.3
  282.3 0.8 multiply_add_fusion
  283.1 1.0 convolution_convert_fusion.5
  284.1 1.1 convolution_convert_fusion.3
  285.2 1.8 copy.52
  287.0 0.3 reduce-scatter.8.cloned.1.call-start
  287.3 1.5 multiply_reduce_fusion
  288.8 0.4 multiply_convert_fusion
  289.3 0.4 fusion.22
  289.7 0.3 fusion.23
  290.0 0.4 convolution_bitcast_fusion
  290.4 0.2 maximum_convert_fusion
  290.5 1.9 convolution_convert_fusion.1
  292.5 8.0 convolution_convert_fusion
  300.6 8.1 convert_bitcast_fusion
  308.7 0.5 convolution_convert_fusion.6
  309.1 0.8 copy.63
  310.0 20.6 %reduce-scatter.8.cloned.1.call-done = bf16[256,1536]{1,0:T(8,128)(2,1)} async-done(((bf16[512,1536]{1,0:T(8,128)(2,1)}), bf16[256,1536]{1,0:T(8,128)(2,1)}) %reduce-scatter.8.cloned.1.call-update) | async-done | bytes 786448 | tf_op jit(solution)/shard_map/reduce_scatter | solution.py:193
  330.6 102.0 %reduce-scatter.14.cloned.1.call-done = bf16[4,1024,512]{2,1,0:T(8,128)(2,1)} async-done(((bf16[4,2048,512]{2,1,0:T(8,128)(2,1)}), bf16[4,1024,512]{2,1,0:T(8,128)(2,1)}) %reduce-scatter.14.cloned.1.call-update) | async-done | bytes 4194320 | tf_op jit(solution)/shard_map/reduce_scatter | solution.py:208
  432.7 102.1 %reduce-scatter.12.cloned.1.call-done = bf16[4,256,2048]{1,2,0:T(8,128)(2,1)} async-done(((bf16[4,512,2048]{1,2,0:T(8,128)(2,1)}), bf16[4,256,2048]{1,2,0:T(8,128)(2,1)}) %reduce-scatter.12.cloned.1.call-update) | async-done | bytes 4194320 | tf_op jit(solution)/shard_map/reduce_scatter | solution.py:205
  534.8 6.2 copy.56
  541.1 0.6 dynamic-slice
  542.3 0.8 fusion.42
  543.1 4.9 all-reduce.4
  548.2 0.9 fusion.57
  549.1 0.9 copy.64
  550.1 33.8 %all-reduce.2 = (bf16[256]{0:T(256)(128)(2,1)S(1)}, bf16[256]{0:T(256)(128)(2,1)S(1)}, bf16[256,4]{0,1:T(4,128)(2,1)S(1)}) all-reduce(bf16[256]{0:T(256)(128)(2,1)S(1)} %dynamic-slice.1, bf16[256]{0:T(256)(128)(2,1)S(1)} %dynamic-slice.3, bf16[256,4]{0,1:T(4,128)(2,1)S(1)} %copy.64), channel_id=1, replica_groups=mesh['rep'=16,'shard'=2] {'rep'}, use_global_device_ids=true, to_apply=%region_22.0 | all-reduce | flops 1536 | bytes 6144 | tf_op jit(solution)/shard_map/psum | solution.py:213
  583.9 0.6 convert_element_type.204
  584.4 0.6 convert_element_type.212
  585.0 0.6 convert_element_type.214
  585.6 91.7 %all-reduce.7.cloned.1.call-done = (bf16[256,1536]{1,0:T(8,128)(2,1)}, bf16[256,512]{1,0:T(8,128)(2,1)}, bf16[4,1024,512]{2,1,0:T(8,128)(2,1)}) async-done(((bf16[256,1536]{1,0:T(8,128)(2,1)}, bf16[256,512]{1,0:T(8,128)(2,1)}, bf16[4,1024,512]{2,1,0:T(8,128)(2,1)}), (bf16[256,1536]{1,0:T(8,128)(2,1)}, bf16[256,512]{1,0:T(8,128)(2,1)}, bf16[4,1024,512]{2,1,0:T(8,128)(2,1)})) %all-reduce.7.cloned.1.call-update) | async-done | bytes 5242896 | tf_op jit(solution)/shard_map/psum | solution.py:214
  677.2 1.8 convert_element_type.210
  679.0 2.5 convert_element_type.208
  681.5 8.8 convert_element_type.219
  690.3 315.0 %all-gather.14.cloned.1.call-done = bf16[64,256,2048]{2,1,0:T(8,128)(2,1)} async-done(((bf16[4,256,2048]{2,1,0:T(8,128)(2,1)}), bf16[64,256,2048]{2,1,0:T(8,128)(2,1)}) %all-gather.14.cloned.1.call-update) | async-done | bytes 67108880 | tf_op jit(solution)/shard_map/all_gather | solution.py:16
  1005.3 23.8 %reduce_sum.240 = bf16[4,256,2048]{2,1,0:T(8,128)(2,1)} reduce(bf16[16,4,256,2048]{3,2,1,0:T(8,128)(2,1)} %bitcast.36, bf16[]{:T(256)} %constant.88.clone.1), dimensions={0}, to_apply=%region_33.0 | reduce | flops 31457280 | bytes 71303168 | tf_op jit(solution)/shard_map/reduce_sum | solution.py:17
  1029.1 6.2 copy.65
  1035.3 6.9 copy.58
  (73 shorter events, 1.0 us)
Async XLA Ops:
  7.2 2.3 copy-start
  7.2 2.4 copy-start.13
  7.2 7.6 copy-start.14
  7.2 11.9 %copy-start.12 = (bf16[256,4]{0,1:T(4,128)(2,1)S(1)}, bf16[256,4]{0,1:T(4,128)(2,1)}, u32[]{:S(2)}) copy-start(bf16[256,4]{0,1:T(4,128)(2,1)} %param.15) | copy-start | bytes 6148
  7.2 16.4 %copy-start.10 = (bf16[256,512]{1,0:T(8,128)(2,1)S(1)}, bf16[256,512]{1,0:T(8,128)(2,1)}, u32[]{:S(2)}) copy-start(bf16[256,512]{1,0:T(8,128)(2,1)} %param.13) | copy-start | bytes 786436
  7.2 30.5 %copy-start.8 = (bf16[1,197,512]{2,1,0:T(8,128)(2,1)S(1)}, bf16[1,197,512]{2,1,0:T(8,128)(2,1)}, u32[]{:S(2)}) copy-start(bf16[1,197,512]{2,1,0:T(8,128)(2,1)} %param.19) | copy-start | bytes 605188
  7.2 38.0 %all-gather.8.cloned.1.call-start = ((), (), s32[]{:S(2)}) async-start(), calls=%async_computation.5 | async-start | bytes 2359296 | tf_op jit(solution)/shard_map/all_gather | solution.py:113
  8.0 142.8 %all-gather.10.cloned.1.call-start = ((), (), s32[]{:S(2)}) async-start(), calls=%async_computation.6 | async-start | bytes 12582912 | tf_op jit(solution)/shard_map/all_gather | solution.py:117
  8.7 247.7 %all-gather.12.cloned.1.call-start = ((), (), s32[]{:S(2)}) async-start(), calls=%async_computation.7 | async-start | bytes 12582912 | tf_op jit(solution)/shard_map/all_gather | solution.py:118
  9.5 300.6 %reduce-scatter.10.cloned.1.call-start = ((), (), s32[]{:S(2)}) async-start(), calls=%async_computation.9 | async-start | bytes 786432 | tf_op jit(solution)/shard_map/reduce_scatter | solution.py:196
  23.7 27.7 %copy-start.11 = (s32[1,197,2]{1,2,0:T(2,128)S(1)}, s32[1,197,2]{1,2,0:T(2,128)}, u32[]{:S(2)}) copy-start(s32[1,197,2]{1,2,0:T(2,128)} %param.18) | copy-start | bytes 4732
  48.6 0.7 copy-start.3
  51.5 204.9 %copy-start.6 = (f32[197,512]{1,0:T(8,128)S(1)}, f32[197,512]{1,0:T(8,128)}, u32[]{:S(2)}) copy-start(f32[197,512]{1,0:T(8,128)} %bitcast_convert_fusion) | copy-start | bytes 1210372
  274.2 7.5 copy-start.1
  274.2 8.1 copy-start.9
  274.2 8.9 copy-start.2
  274.2 9.9 copy-start.4
  287.0 43.6 %reduce-scatter.8.cloned.1.call-start = ((), (), s32[]{:S(2)}) async-start(), calls=%async_computation.8 | async-start | bytes 2359296 | tf_op jit(solution)/shard_map/reduce_scatter | solution.py:193
  287.3 2.7 copy-start.5
  292.5 140.1 %reduce-scatter.14.cloned.1.call-start = ((), (), s32[]{:S(2)}) async-start(), calls=%async_computation.11 | async-start | bytes 12582912 | tf_op jit(solution)/shard_map/reduce_scatter | solution.py:208
  300.5 234.3 %reduce-scatter.12.cloned.1.call-start = ((), (), s32[]{:S(2)}) async-start(), calls=%async_computation.10 | async-start | bytes 12582912 | tf_op jit(solution)/shard_map/reduce_scatter | solution.py:205
  308.6 240.5 %reduce-scatter.16.cloned.1.call-start = ((), (), s32[]{:S(2)}) async-start(), calls=%async_computation.13 | async-start | bytes 196608
  310.0 367.3 %all-reduce.7.cloned.1.call-start = ((), (), s32[]{:S(2)}) async-start(), calls=%async_computation.14 | async-start | bytes 10485760 | tf_op jit(solution)/shard_map/psum | solution.py:214
  432.6 108.4 %copy-start.15 = (u32[32]{0:T(128)S(1)}, u32[32]{0:T(128)}, u32[]{:S(2)}) copy-start(u32[32]{0:T(128)} %constant.94) | copy-start | bytes 388
  432.6 109.7 %copy-start.7 = (bf16[512,1536]{1,0:T(8,128)(2,1)S(1)}, bf16[512,1536]{1,0:T(8,128)(2,1)}, u32[]{:S(2)}) copy-start(bf16[512,1536]{1,0:T(8,128)(2,1)} %all-gather.8.cloned.1.call-done) | copy-start | bytes 4718596
  432.6 572.7 %all-gather.14.cloned.1.call-start = ((), (), s32[]{:S(2)}) async-start(), calls=%async_computation.12 | async-start | bytes 71303168 | tf_op jit(solution)/shard_map/all_gather | solution.py:16
Sparse Core Ops, SparseCore 0:
  9.6 35.5 all-gather.7
  46.7 103.9 all-gather.9
  152.3 103.9 all-gather.11
  287.1 14.5 reduce-scatter.9
  304.5 26.0 reduce-scatter.7
  333.3 99.2 reduce-scatter.13
  435.6 99.2 reduce-scatter.11
  537.0 10.2 reduce-scatter.15
  551.4 125.7 all-reduce.6
  679.3 325.9 all-gather.13
